TPU v7x, 32 devices: a whole 2x2x4 slice. The times are simulated.
32 devices in a mesh: parts: 2 (over y), space: 4 (over z), filt: 2 (over x), rep: 2 (over core).
Axes of the slice: x: 2, y: 2, z: 4, core: 2. Of those that a mesh axis runs over, the one named last changes fastest.
Arguments:
- features: bfloat16 [128, 512, 256], P(('parts', 'space'), 'filt', 'rep'), parts along dimension 0, may hold values from -6 to 6
- kernel: bfloat16 [3, 3, 512, 512], P(None, None, 'filt'), may hold values from -0.09375 to 0.09375
- shift_bias: float32 [512], P('filt'), may hold values from -3 to 3
- upstream: bfloat16 [128, 512, 256], P(('parts', 'space'), 'filt', 'rep'), parts along dimension 0, may hold values from -6 to 6
Outputs:
- block_out: bfloat16 [128, 512, 256], P(('parts', 'space'), 'filt', 'rep'), parts along dimension 0
- input_grad: bfloat16 [128, 512, 256], P(('parts', 'space'), 'filt', 'rep'), parts along dimension 0
- kernel_grad: float32 [6, 3, 512, 512], P('parts', None, 'filt'), parts along dimension 0
- bias_grad: float32 [1024], P(('parts', 'filt')), parts along dimension 0
There are 2 independent parts, one for each index of `parts`. A program takes and returns all parts, laid end to end along the dimension named above; an argument that names none is the same for every part. Nothing has to cross between parts.
All inputs are finite; a program needn't handle non-finite values.
Results may differ from a plain program's by a relative error of at most 0.0055.
Values may be sent and summed in bfloat16 or wider, within the bound.
No kernel may reach another device: no remote copies, remote signals or barrier semaphores. Data moves between devices by JAX's collectives and lax.ppermute only.
A program may use at most 64 MiB of HBM per device.

v0:
```python
import jax
import jax.numpy as jnp
from jax import lax
from jax.sharding import PartitionSpec as P


def padded(cells, sides, width):
    for axis, dim in sides:
        count = lax.axis_size(axis)
        ends = count - 1
        head = lax.slice_in_dim(cells, 0, width, axis=dim)
        tail = lax.slice_in_dim(cells, cells.shape[dim] - width, cells.shape[dim], axis=dim)
        cells = jnp.concatenate(
            [
                lax.ppermute(tail, axis, [(i, (i + 1) % count) for i in range(ends)]),
                cells,
                lax.ppermute(head, axis, [((i + 1) % count, i) for i in range(ends)]),
            ],
            axis=dim,
        )
    return cells


def forward_taps(running, panels, kernel, band_rows, band_cols):
    for row_tap in range(3):
        for col_tap in range(3):
            window = panels[row_tap : row_tap + band_rows, :, col_tap : col_tap + band_cols]
            weights = kernel[row_tap, col_tap]
            running = running + jnp.einsum(
                "oc,hcw->how", weights, window, preferred_element_type=jnp.float32
            )
    return running


def weight_taps(panels, slope, band_rows, band_cols):
    rows_out = []
    for row_tap in range(3):
        taps_row = []
        for col_tap in range(3):
            window = panels[row_tap : row_tap + band_rows, :, col_tap : col_tap + band_cols]
            taps_row.append(
                jnp.einsum("how,hcw->oc", slope, window, preferred_element_type=jnp.float32)
            )
        rows_out.append(jnp.stack(taps_row))
    return jnp.stack(rows_out)


def backward_taps(slope_pad, weights, band_rows, band_cols):
    summed = jnp.zeros((band_rows, weights.shape[3], band_cols), jnp.float32)
    for row_tap in range(3):
        for col_tap in range(3):
            part_slope = slope_pad[
                2 - row_tap : 2 - row_tap + band_rows, :, 2 - col_tap : 2 - col_tap + band_cols
            ]
            summed = summed + jnp.einsum(
                "oc,how->hcw",
                weights[row_tap, col_tap],
                part_slope,
                preferred_element_type=jnp.float32,
            )
    return summed


def per_device(features, kernel, shift_bias, upstream):
    band_rows, local_out, band_cols = upstream.shape
    rimmed = padded(features, (("space", 0), ("rep", 2)), 1)
    start_pre = (
        jnp.zeros((band_rows, local_out, band_cols), jnp.float32) + shift_bias[None, :, None]
    )
    all_panels = lax.all_gather(rimmed, "filt", axis=1, tiled=True)
    pre = forward_taps(start_pre, all_panels, kernel, band_rows, band_cols)
    sigm = jax.nn.sigmoid(pre)
    block_out = (features.astype(jnp.float32) + pre * sigm).astype(jnp.bfloat16)
    slope = (upstream.astype(jnp.float32) * sigm * (1.0 + pre * (1.0 - sigm))).astype(jnp.bfloat16)
    kernel_part = weight_taps(all_panels, slope, band_rows, band_cols)
    slope_pad = padded(slope, (("space", 0), ("rep", 2)), 1)
    slope_all = lax.all_gather(slope_pad, "filt", axis=1, tiled=True)
    own_rows = lax.all_to_all(kernel, "filt", split_axis=3, concat_axis=2, tiled=True)
    back = backward_taps(slope_all, own_rows, band_rows, band_cols)
    input_grad = (upstream.astype(jnp.float32) + back).astype(jnp.bfloat16)
    bias_part = jnp.sum(slope.astype(jnp.float32), axis=(0, 2))
    kernel_sum, bias_sum = lax.psum((kernel_part, bias_part), ("space", "rep"))
    total_cells = band_rows * band_cols * lax.axis_size("space") * lax.axis_size("rep")
    scale = 1.0 / jnp.sqrt(jnp.float32(total_cells))
    return (block_out, input_grad, kernel_sum * scale, bias_sum * scale)


def solution(mesh):
    in_specs = (
        P(("parts", "space"), "filt", "rep"),
        P(None, None, "filt", None),
        P("filt"),
        P(("parts", "space"), "filt", "rep"),
    )
    out_specs = (
        P(("parts", "space"), "filt", "rep"),
        P(("parts", "space"), "filt", "rep"),
        P("parts", None, "filt", None),
        P(("parts", "filt")),
    )
    return jax.shard_map(
        per_device, mesh=mesh, in_specs=in_specs, out_specs=out_specs, check_vma=False
    )
```

profile of v0, /device:TPU:0, one launch (start us, length us, event | category | flops | bytes accessed | tf_op | source)
XLA Modules:
  0.0 250.9 jit_solution(6216047578776951642)
XLA Ops:
  7.2 0.0 all-gather.3.cloned.1.call-start
  7.2 1.5 copy.34
  8.7 1.3 collective-permute-start.1
  10.0 5.6 %collective-permute-start = (bf16[1,256,128]{1,2,0:T(8,128)(2,1)S(1)}, bf16[1,256,128]{1,2,0:T(8,128)(2,1)S(1)}, u32[]{:S(2)}, u32[]{:S(2)}) collective-permute-start(bf16[1,256,128]{1,2,0:T(8,128)(2,1)S(1)} %get-tuple-element.21), channel_id=1, source_target_pairs={{0,4},{4,8},{8,12},{1,5},{5,9},{9,13},{2,6},{6,10},{10,14},{3,7},{... | collective-permute-start | bytes 196616 | tf_op jit(solution)/shard_map/ppermute | solution.py:15
  15.6 0.3 collective-permute-done.1
  15.9 1.6 collective-permute-done
  17.6 1.4 collective-permute-start.3
  19.0 3.0 %collective-permute-start.2 = (bf16[18,256,1]{1,2,0:T(2,128)(2,1)S(1)}, bf16[18,256,1]{1,2,0:T(2,128)(2,1)S(1)}, u32[]{:S(2)}, u32[]{:S(2)}) collective-permute-start(bf16[18,256,1]{1,2,0:T(2,128)(2,1)S(1)} %get-tuple-element.17), channel_id=1, source_target_pairs={{0,1},{2,3},{4,5},{6,7},{8,9},{10,11},{12,13},{14,15},{16,17},{18,... | collective-permute-start | bytes 27656 | tf_op jit(solution)/shard_map/ppermute | solution.py:15
  22.0 0.8 collective-permute-done.2
  22.8 1.7 pad_maximum_fusion.1
  24.6 0.0 all-reduce.2.cloned.1.call-start
  24.6 0.5 copy.38
  25.2 39.7 %all-gather.3.cloned.1.call-done = bf16[18,512,130]{1,2,0:T(8,128)(2,1)} async-done(((bf16[18,256,130]{1,2,0:T(8,128)(2,1)}), bf16[18,512,130]{1,2,0:T(8,128)(2,1)}) %all-gather.3.cloned.1.call-update) | async-done | bytes 2396176 | tf_op jit(solution)/shard_map/all_gather | solution.py:70
  64.9 2.5 %fusion.33 = f32[16,128,256]{2,1,0:T(8,128)S(1)} fusion(bf16[18,512,130]{1,2,0:T(8,128)(2,1)} %all-gather.3.cloned.1.call-done, bf16[3,3,256,512]{3,2,1,0:T(8,128)(2,1)} %param.5), kind=kOutput, calls=%fused_computation.42 | convolution fusion | flops 536870912 | bytes 4456448 | tf_op jit(solution)/shard_map/oc,hcw->how/dot_general | solution.py:29
  67.4 0.6 copy-done.2
  68.1 0.7 fusion.37
  68.8 0.8 fusion.41
  69.6 0.8 fusion.45
  70.3 0.7 fusion.49
  71.1 0.8 fusion.53
  71.8 0.8 fusion.57
  72.6 0.7 fusion.61
  73.4 3.4 %convert_reduce_fusion = (f32[256]{0:T(256)S(1)}, bf16[16,256,128]{1,2,0:T(8,128)(2,1)S(1)}, bf16[16,256,128]{1,2,0:T(8,128)(2,1)}) fusion(bf16[16,256,128]{1,2,0:T(8,128)(2,1)S(1)} %copy.38, bf16[16,256,128]{1,2,0:T(8,128)(2,1)S(1)} %copy.34, bf16[3,3,256,512]{3,2,1,0:T(8,128)(2,1)S(1)} %copy-done.2, bf16[18,512,130]{1,2,0:T(8,128)(2,1)S(1)} %copy-done, ...), kind=kOutput, calls=%fused_computation.35 | convolution fusion | flops 549977856 | bytes 23332864 | tf_op jit(solution)/shard_map/oc,hcw->how/dot_general | solution.py:29
  76.8 0.8 fusion.91
  77.6 0.8 fusion.88
  78.3 0.7 fusion.85
  79.1 0.1 maximum_bitcast_fusion.2
  79.2 0.8 fusion.73
  80.0 0.8 fusion.70
  80.8 0.7 fusion.67
  81.5 0.8 fusion.82
  82.3 0.8 fusion.79
  83.0 0.7 fusion.76
  83.8 0.6 maximum_bitcast_fusion
  84.3 2.7 %pad_maximum_fusion = f32[3,3,256,512]{3,2,1,0:T(8,128)} fusion(f32[1,3,256,512]{3,2,1,0:T(8,128)S(1)} %maximum_bitcast_fusion.2, f32[1,3,256,512]{3,2,1,0:T(8,128)S(1)} %get-tuple-element.24, f32[1,3,256,512]{3,2,1,0:T(8,128)S(1)} %get-tuple-element.23), kind=kLoop, calls=%fused_computation | loop fusion | flops 2359296 | bytes 9437184 | tf_op jit(solution)/shard_map/stack | solution.py:45
  87.1 0.0 all-gather.5.cloned.1.call-start
  87.1 1.3 collective-permute-start.5
  88.4 4.5 %collective-permute-start.4 = (bf16[1,256,128]{1,2,0:T(8,128)(2,1)S(1)}, bf16[1,256,128]{1,2,0:T(8,128)(2,1)S(1)}, u32[]{:S(2)}, u32[]{:S(2)}) collective-permute-start(bf16[1,256,128]{1,2,0:T(8,128)(2,1)S(1)} %get-tuple-element.19), channel_id=1, source_target_pairs={{0,4},{4,8},{8,12},{1,5},{5,9},{9,13},{2,6},{6,10},{10,14},{3,7},{... | collective-permute-start | bytes 196616 | tf_op jit(solution)/shard_map/ppermute | solution.py:15
  93.0 0.3 collective-permute-done.5
  93.3 3.0 %collective-permute-done.4 = bf16[1,256,128]{1,2,0:T(8,128)(2,1)S(1)} collective-permute-done((bf16[1,256,128]{1,2,0:T(8,128)(2,1)S(1)}, bf16[1,256,128]{1,2,0:T(8,128)(2,1)S(1)}, u32[]{:S(2)}, u32[]{:S(2)}) %collective-permute-start.4) | collective-permute-done | bytes 65568 | tf_op jit(solution)/shard_map/ppermute | solution.py:15
  96.4 1.4 collective-permute-start.7
  97.8 3.0 %collective-permute-start.6 = (bf16[18,256,1]{1,2,0:T(2,128)(2,1)S(1)}, bf16[18,256,1]{1,2,0:T(2,128)(2,1)S(1)}, u32[]{:S(2)}, u32[]{:S(2)}) collective-permute-start(bf16[18,256,1]{1,2,0:T(2,128)(2,1)S(1)} %get-tuple-element.15), channel_id=1, source_target_pairs={{0,1},{2,3},{4,5},{6,7},{8,9},{10,11},{12,13},{14,15},{16,17},{18,... | collective-permute-start | bytes 27656 | tf_op jit(solution)/shard_map/ppermute | solution.py:15
  100.8 0.8 collective-permute-done.6
  101.7 1.7 pad_maximum_fusion.2
  103.4 3.8 %copy.39 = bf16[3,3,256,512]{2,1,0,3:T(4,128)(2,1)} copy(bf16[3,3,256,512]{3,2,1,0:T(8,128)(2,1)S(1)} %copy-done.3) | data formatting | bytes 4718592 | tf_op args[1]
  107.2 40.8 %all_to_all.18 = bf16[3,3,256,512]{2,1,0,3:T(4,128)(2,1)S(1)} all-to-all(bf16[3,3,256,512]{2,1,0,3:T(4,128)(2,1)} %copy.39), channel_id=1, replica_groups=mesh['parts'=2,'space'=4,'filt'=2,'rep'=2] {'filt'}, dimensions={3} | all-to-all | bytes 4718592 | tf_op jit(solution)/shard_map/all_to_all | solution.py:78
  148.0 3.6 %copy.40 = bf16[3,3,256,2,256]{4,2,3,1,0:T(8,128)(2,1)} copy(bf16[3,3,256,2,256]{2,1,0,4,3:T(4,128)(2,1)S(1)} %bitcast.163) | data formatting | bytes 4718592 | tf_op jit(solution)/shard_map/all_to_all | solution.py:78
  151.6 2.3 copy.59
  153.9 17.7 %psum.15 = f32[256]{0:T(256)S(1)} all-reduce(f32[256]{0:T(256)S(1)} %get-tuple-element.12), channel_id=1, replica_groups=mesh['parts'=2,'space'=4,'filt'=2,'rep'=2] {'space','rep'}, use_global_device_ids=true, to_apply=%region_2.0 | all-reduce | flops 256 | bytes 2048 | tf_op jit(solution)/shard_map/psum | solution.py:82
  171.6 0.6 broadcast_multiply_fusion.1
  172.1 22.5 %all-reduce.2.cloned.1.call-done = f32[3,3,256,512]{3,2,1,0:T(8,128)} async-done(((f32[3,3,256,512]{3,2,1,0:T(8,128)}), f32[3,3,256,512]{3,2,1,0:T(8,128)}) %all-reduce.2.cloned.1.call-update) | async-done | bytes 4718608 | tf_op jit(solution)/shard_map/psum | solution.py:82
  194.6 5.3 %broadcast_multiply_fusion = f32[3,3,256,512]{3,2,1,0:T(8,128)} fusion(f32[3,3,256,512]{3,2,1,0:T(8,128)} %all-reduce.2.cloned.1.call-done), kind=kLoop, calls=%fused_computation.3 | loop fusion | flops 1179648 | bytes 9437184 | tf_op jit(solution)/shard_map/mul | solution.py:85
  199.9 34.0 %all-gather.5.cloned.1.call-done = bf16[18,512,130]{1,2,0:T(8,128)(2,1)} async-done(((bf16[18,256,130]{1,2,0:T(8,128)(2,1)}), bf16[18,512,130]{1,2,0:T(8,128)(2,1)}) %all-gather.5.cloned.1.call-update) | async-done | bytes 2396176 | tf_op jit(solution)/shard_map/all_gather | solution.py:77
  233.9 2.5 fusion.5
  236.4 0.7 fusion.7
  237.2 0.7 fusion.9
  237.9 0.7 fusion.11
  238.6 0.7 fusion.13
  239.3 0.7 fusion.15
  240.0 0.7 fusion.19
  240.8 0.7 fusion.17
  241.5 0.5 copy-done.6
  242.0 1.1 fusion.2
  243.1 1.3 copy.60
  (25 shorter events, 0.2 us)
Async XLA Ops:
  7.2 57.7 %all-gather.3.cloned.1.call-start = ((), (), s32[]{:S(2)}) async-start(), calls=%async_computation.1 | async-start | bytes 3760128 | tf_op jit(solution)/shard_map/all_gather | solution.py:70
  8.7 7.2 %collective-permute-start.1 = (bf16[1,256,128]{1,2,0:T(8,128)(2,1)S(1)}, bf16[1,256,128]{1,2,0:T(8,128)(2,1)S(1)}, u32[]{:S(2)}, u32[]{:S(2)}) collective-permute-start(bf16[1,256,128]{1,2,0:T(8,128)(2,1)S(1)} %get-tuple-element.22), channel_id=1, source_target_pairs={{4,0},{8,4},{12,8},{5,1},{9,5},{13,9},{6,2},{10,6},{14,10},{7,3},{... | collective-permute-start | bytes 196616 | tf_op jit(solution)/shard_map/ppermute | solution.py:17
  10.0 7.5 %collective-permute-start = (bf16[1,256,128]{1,2,0:T(8,128)(2,1)S(1)}, bf16[1,256,128]{1,2,0:T(8,128)(2,1)S(1)}, u32[]{:S(2)}, u32[]{:S(2)}) collective-permute-start(bf16[1,256,128]{1,2,0:T(8,128)(2,1)S(1)} %get-tuple-element.21), channel_id=1, source_target_pairs={{0,4},{4,8},{8,12},{1,5},{5,9},{9,13},{2,6},{6,10},{10,14},{3,7},{... | collective-permute-start | bytes 196616 | tf_op jit(solution)/shard_map/ppermute | solution.py:15
  17.5 7.1 %copy-start.7 = (bf16[16,256,128]{2,1,0:T(8,128)(2,1)S(1)}, bf16[16,256,128]{2,1,0:T(8,128)(2,1)}, u32[]{:S(2)}) copy-start(bf16[16,256,128]{2,1,0:T(8,128)(2,1)} %param.7) | copy-start | bytes 3145732
  17.6 4.5 %collective-permute-start.3 = (bf16[18,256,1]{1,2,0:T(2,128)(2,1)S(1)}, bf16[18,256,1]{1,2,0:T(2,128)(2,1)S(1)}, u32[]{:S(2)}, u32[]{:S(2)}) collective-permute-start(bf16[18,256,1]{1,2,0:T(2,128)(2,1)S(1)} %get-tuple-element.18), channel_id=1, source_target_pairs={{1,0},{3,2},{5,4},{7,6},{9,8},{11,10},{13,12},{15,14},{17,16},{19,... | collective-permute-start | bytes 27656 | tf_op jit(solution)/shard_map/ppermute | solution.py:17
  19.0 3.9 %collective-permute-start.2 = (bf16[18,256,1]{1,2,0:T(2,128)(2,1)S(1)}, bf16[18,256,1]{1,2,0:T(2,128)(2,1)S(1)}, u32[]{:S(2)}, u32[]{:S(2)}) collective-permute-start(bf16[18,256,1]{1,2,0:T(2,128)(2,1)S(1)} %get-tuple-element.17), channel_id=1, source_target_pairs={{0,1},{2,3},{4,5},{6,7},{8,9},{10,11},{12,13},{14,15},{16,17},{18,... | collective-permute-start | bytes 27656 | tf_op jit(solution)/shard_map/ppermute | solution.py:15
  24.6 170.0 %all-reduce.2.cloned.1.call-start = ((), (), s32[]{:S(2)}) async-start(), calls=%async_computation.3 | async-start | bytes 9437184 | tf_op jit(solution)/shard_map/psum | solution.py:82
  25.2 48.2 %copy-start.5 = (bf16[16,256,128]{1,2,0:T(8,128)(2,1)}, bf16[16,256,128]{1,2,0:T(8,128)(2,1)S(1)}, u32[]{:S(2)}) copy-start(bf16[16,256,128]{1,2,0:T(8,128)(2,1)S(1)} %copy.38) | copy-start | bytes 3145732
  64.9 2.5 %copy-start = (bf16[18,512,130]{1,2,0:T(8,128)(2,1)S(1)}, bf16[18,512,130]{1,2,0:T(8,128)(2,1)}, u32[]{:S(2)}) copy-start(bf16[18,512,130]{1,2,0:T(8,128)(2,1)} %all-gather.3.cloned.1.call-done) | copy-start | bytes 7188484
  64.9 3.2 %copy-start.2 = (bf16[3,3,256,512]{3,2,1,0:T(8,128)(2,1)S(1)}, bf16[3,3,256,512]{3,2,1,0:T(8,128)(2,1)}, u32[]{:S(2)}) copy-start(bf16[3,3,256,512]{3,2,1,0:T(8,128)(2,1)} %param.5) | copy-start | bytes 7077892
  72.6 0.8 copy-start.8
  87.1 146.9 %all-gather.5.cloned.1.call-start = ((), (), s32[]{:S(2)}) async-start(), calls=%async_computation.2 | async-start | bytes 3760128 | tf_op jit(solution)/shard_map/all_gather | solution.py:77
  87.1 6.2 %collective-permute-start.5 = (bf16[1,256,128]{1,2,0:T(8,128)(2,1)S(1)}, bf16[1,256,128]{1,2,0:T(8,128)(2,1)S(1)}, u32[]{:S(2)}, u32[]{:S(2)}) collective-permute-start(bf16[1,256,128]{1,2,0:T(8,128)(2,1)S(1)} %get-tuple-element.20), channel_id=1, source_target_pairs={{4,0},{8,4},{12,8},{5,1},{9,5},{13,9},{6,2},{10,6},{14,10},{7,3},{... | collective-permute-start | bytes 196616 | tf_op jit(solution)/shard_map/ppermute | solution.py:17
  88.4 7.9 %collective-permute-start.4 = (bf16[1,256,128]{1,2,0:T(8,128)(2,1)S(1)}, bf16[1,256,128]{1,2,0:T(8,128)(2,1)S(1)}, u32[]{:S(2)}, u32[]{:S(2)}) collective-permute-start(bf16[1,256,128]{1,2,0:T(8,128)(2,1)S(1)} %get-tuple-element.19), channel_id=1, source_target_pairs={{0,4},{4,8},{8,12},{1,5},{5,9},{9,13},{2,6},{6,10},{10,14},{3,7},{... | collective-permute-start | bytes 196616 | tf_op jit(solution)/shard_map/ppermute | solution.py:15
  96.4 7.1 %copy-start.3 = (bf16[3,3,256,512]{3,2,1,0:T(8,128)(2,1)S(1)}, bf16[3,3,256,512]{3,2,1,0:T(8,128)(2,1)}, u32[]{:S(2)}) copy-start(bf16[3,3,256,512]{3,2,1,0:T(8,128)(2,1)} %param.5) | copy-start | bytes 7077892
  96.4 4.5 %collective-permute-start.7 = (bf16[18,256,1]{1,2,0:T(2,128)(2,1)S(1)}, bf16[18,256,1]{1,2,0:T(2,128)(2,1)S(1)}, u32[]{:S(2)}, u32[]{:S(2)}) collective-permute-start(bf16[18,256,1]{1,2,0:T(2,128)(2,1)S(1)} %get-tuple-element.16), channel_id=1, source_target_pairs={{1,0},{3,2},{5,4},{7,6},{9,8},{11,10},{13,12},{15,14},{17,16},{19,... | collective-permute-start | bytes 27656 | tf_op jit(solution)/shard_map/ppermute | solution.py:17
  97.8 3.9 %collective-permute-start.6 = (bf16[18,256,1]{1,2,0:T(2,128)(2,1)S(1)}, bf16[18,256,1]{1,2,0:T(2,128)(2,1)S(1)}, u32[]{:S(2)}, u32[]{:S(2)}) collective-permute-start(bf16[18,256,1]{1,2,0:T(2,128)(2,1)S(1)} %get-tuple-element.15), channel_id=1, source_target_pairs={{0,1},{2,3},{4,5},{6,7},{8,9},{10,11},{12,13},{14,15},{16,17},{18,... | collective-permute-start | bytes 27656 | tf_op jit(solution)/shard_map/ppermute | solution.py:15
  172.1 61.8 %copy-start.4 = (bf16[3,3,256,2,256]{4,2,3,1,0:T(8,128)(2,1)S(1)}, bf16[3,3,256,2,256]{4,2,3,1,0:T(8,128)(2,1)}, u32[]{:S(2)}) copy-start(bf16[3,3,256,2,256]{4,2,3,1,0:T(8,128)(2,1)} %copy.40) | copy-start | bytes 7077892
  233.9 2.5 copy-start.1
  240.8 1.2 copy-start.6
Sparse Core Ops, SparseCore 0:
  24.7 40.1 all-gather.2
  87.2 107.3 all-reduce.1
  196.2 37.7 all-gather.4
where the time goes:
time: 251 us
  waiting for transfers between devices  103 us (41%)
  blocking collectives  58.5 us (23%)
  matrix products  26.5 us (11%)
  starting transfers between devices  21.7 us (9%)
  local copies, waits for them, and re-layouts  14.2 us (6%)
  between operations  14.2 us (6%)
  other arithmetic  12.8 us (5%)
    all_to_all x1, blocking collectives, per_device(): lax.all_to_all(kernel, 'filt', split_axis=3, concat_axis=2, tiled=True)  40.8 us
    all_gather x1, waiting for transfers between devices, per_device(): all_panels = lax.all_gather(rimmed, 'filt', axis=1, tiled=True)  39.7 us
    all_gather x1, waiting for transfers between devices, per_device(): slope_all = lax.all_gather(slope_pad, 'filt', axis=1, tiled=True)  34 us
    psum x1, waiting for transfers between devices, per_device(): kernel_sum, bias_sum = lax.psum((kernel_part, bias_part), ('space', 'rep'))  22.5 us
    psum x1, blocking collectives, per_device(): kernel_sum, bias_sum = lax.psum((kernel_part, bias_part), ('space', 'rep'))  17.7 us
    ppermute x4, starting transfers between devices, padded(): lax.ppermute(tail, axis, [(i, (i + 1) % count) for i in range(ends)])  16.2 us
    dot_general x9, matrix products, forward_taps(): jnp.einsum('oc,hcw->how', weights, window, preferred_element_type=jnp.flo...  11.2 us
    unnamed x23, local copies, waits for them, and re-layouts  10.5 us
  transfers between devices with their start and end apart: 11, of which 9 were waited for; matrix products, arithmetic and copies ran while one was open for 7% of the time, Pallas kernels for 0%

commit v1 on v0

v1 whole, which is shorter than its diff:
```python
import functools

import jax
import jax.numpy as jnp
from jax import lax
from jax.experimental import pallas as pl
from jax.experimental.pallas import tpu as pltpu
from jax.sharding import PartitionSpec as P

F32 = jnp.float32
BF16 = jnp.bfloat16
LANES = 128
VMEM_BYTES = 40 * 2**20


def shift_perm(count, step):
    return [(i, (i + step) % count) for i in range(count)]


def swap_rep(cells):
    return lax.ppermute(cells, "rep", [(0, 1), (1, 0)])


def send_rows(cells, edge):
    count = lax.axis_size("space")
    down = jnp.concatenate([cells[-1:], edge[None]], axis=0)
    up = jnp.concatenate([cells[:1], edge[None]], axis=0)
    return down, up, [(i, i + 1) for i in range(count - 1)], [(i + 1, i) for i in range(count - 1)]


def edge_kernel(cells, out):
    core = lax.axis_index("rep")
    rows = cells.shape[0]
    lane = lax.broadcasted_iota(jnp.int32, out.shape, 1)
    total = jnp.zeros(out.shape, F32)
    for row in range(rows):
        value = cells[row].astype(F32)
        moved = pltpu.roll(value, row + 2, 1)
        plain = pltpu.roll(value, row + 1, 1)
        total = jnp.where(lane == row + 1, jnp.where(core == 0, moved, plain), total)
    out[...] = total.astype(BF16)


def column_shifts(value, edge, p, core, lane):
    wide = value.astype(F32)
    border = pltpu.roll(edge, LANES - 1 - p + core, 1)
    before = pltpu.roll(wide, 1, 1)
    after = pltpu.roll(wide, LANES - 1, 1)
    none = jnp.zeros_like(border)
    before = jnp.where(lane == 0, jnp.where(core == 1, border, none), before)
    after = jnp.where(lane == LANES - 1, jnp.where(core == 0, border, none), after)
    return before.astype(BF16), after.astype(BF16)


def forward_kernel(runs, rows, cuts, groups, has_sum, last, names, *refs):
    ref = dict(zip(names, refs))
    cells_x, slope_x = ref["cells"], ref["slope_all"]
    core = lax.axis_index("rep")
    mine = lax.axis_index("filt")
    local = ref["features"].shape[1]
    step = pl.program_id(0)

    @pl.when(step == 0)
    def _():
        lane = lax.broadcasted_iota(jnp.int32, (local, LANES), 1)
        for turn in range(groups):
            def source(row):
                if turn == 0:
                    if row < 0:
                        return ref["above"][0], ref["above"][1], rows
                    if row >= rows:
                        return ref["below"][0], ref["below"][1], 1
                    return ref["features"][row], ref["edge"][...], row + 1
                a, b, c, d = [f"{part}{turn}" for part in "abcd"]
                if row < 0:
                    return ref[d][2], ref[d][4], rows
                if row >= rows:
                    return ref[d][1], ref[d][3], 1
                edge = ref[b][cuts[1] - cuts[0]]
                if row < cuts[0]:
                    return ref[a][row], edge, row + 1
                if row < cuts[1]:
                    return ref[b][row - cuts[0]], edge, row + 1
                if row < cuts[2]:
                    return ref[c][row - cuts[1]], edge, row + 1
                return ref[d][0], edge, row + 1

            base = pl.multiple_of(lax.rem(mine + turn, groups) * local, local)
            block = 0
            for start, count in runs:
                for row in range(start - 1, start + count + 1):
                    value, edge, p = source(row)
                    before, after = column_shifts(value, edge.astype(F32), p, core, lane)
                    where = (pl.ds(base, local), pl.ds(block * LANES, LANES))
                    cells_x[(0,) + where] = before
                    cells_x[(1,) + where] = value
                    cells_x[(2,) + where] = after
                    block += 1
        edges = jnp.zeros((local, LANES), F32)
        block, place = 0, 0
        for start, count in runs:
            total = None
            for row_tap in range(3):
                for col_tap in range(3):
                    window = cells_x[
                        col_tap, :, (block + row_tap) * LANES : (block + row_tap + count) * LANES
                    ]
                    term = jnp.dot(
                        ref["kernel"][row_tap, col_tap], window, preferred_element_type=F32
                    )
                    total = term if total is None else total + term
            for at in range(count):
                row = start + at
                pre = total[:, at * LANES : (at + 1) * LANES] + ref["bias"][...]
                sigm = jax.nn.sigmoid(pre)
                out = ref["features"][row].astype(F32) + pre * sigm
                ref["block_out"][place] = out.astype(BF16)
                slope = ref["upstream"][row].astype(F32) * sigm * (1.0 + pre * (1.0 - sigm))
                slope = slope.astype(BF16)
                ref["slope"][place] = slope
                slope_x[:, place * LANES : (place + 1) * LANES] = slope
                wide = slope.astype(F32)
                moved = pltpu.roll(wide, row + 2, 1)
                plain = pltpu.roll(wide, row + 1, 1)
                edges = jnp.where(lane == row + 1, jnp.where(core == 0, moved, plain), edges)
                place += 1
            block += count + 2
        if "edge_in" in ref:
            edges = edges + ref["edge_in"][...].astype(F32)
        ref["edge_out"][...] = edges.astype(BF16)

    def grads(row_tap, col_tap):
        block, place, total = 0, 0, None
        for start, count in runs:
            window = cells_x[
                col_tap, :, pl.ds(pl.multiple_of((block + row_tap) * LANES, LANES), count * LANES)
            ]
            term = lax.dot_general(
                slope_x[:, place * LANES : (place + count) * LANES],
                window,
                (((1,), (1,)), ((), ())),
                preferred_element_type=F32,
            )
            total = term if total is None else total + term
            block += count + 2
            place += count
        return total

    width = slope_x.shape[1]
    bias = lax.dot_general(
        jnp.ones((16, width), BF16), slope_x[...], (((1,), (1,)), ((), ())),
        preferred_element_type=F32,
    )
    if "bias_in" in ref:
        bias = bias + ref["bias_in"][...]
    if not last:
        ref["bias_out"][...] = bias
        for col_tap in range(3):
            total = grads(step, col_tap)
            if has_sum:
                total = total + ref["sum_in"][0, col_tap]
            ref["sum_out"][0, col_tap] = total
        return
    halves = local // 2
    own = pl.multiple_of(core * halves, halves)
    other = pl.multiple_of((1 - core) * halves, halves)
    hold = ref["hold"]
    for tap in range(3):
        @pl.when(step == tap)
        def _():
            for col_tap in range(3):
                hold[...] = grads(tap, col_tap) + ref["sum_in"][0, col_tap]
                at = col_tap * halves
                ref[f"away{tap}"][at : at + halves] = hold[pl.ds(other, halves)].astype(BF16)
                ref[f"keep{tap}"][at : at + halves] = hold[pl.ds(own, halves)]
            if tap == 0:
                at = 3 * halves
                ref["away0"][at:] = jnp.zeros((16, hold.shape[1]), BF16)
                ref["keep0"][at:] = jnp.zeros((16, hold.shape[1]), F32)
                ref["away0"][at:, :local] = bias.astype(BF16)
                ref["keep0"][at:, :local] = bias


def backward_kernel(rows_out, parts, rows, turn, groups, names, *refs):
    ref = dict(zip(names, refs))
    cells_x = ref["cells"]
    core = lax.axis_index("rep")
    local = cells_x.shape[1]
    lane = lax.broadcasted_iota(jnp.int32, (local, LANES), 1)

    def source(row):
        if row < 0:
            return ref["above"][0], ref["above"][1], rows
        if row >= rows:
            return ref["below"][0], ref["below"][1], 1
        for at, held in enumerate(parts):
            if row in held:
                return ref[f"slope{at}"][held.index(row)], ref["edge"][...], row + 1

    target = lax.rem(lax.axis_index("filt") + turn, groups)
    channels = pl.ds(pl.multiple_of(target * local, local), local)
    block, place = 0, 0
    for start, count in rows_out:
        for at, row in enumerate(range(start - 1, start + count + 1)):
            value, edge, p = source(row)
            before, after = column_shifts(value, edge.astype(F32), p, core, lane)
            lanes = pl.ds((block + at) * LANES, LANES)
            cells_x[0, :, lanes] = after
            cells_x[1, :, lanes] = value
            cells_x[2, :, lanes] = before
        total = None
        for row_tap in range(3):
            for col_tap in range(3):
                first = block + 2 - row_tap
                term = jnp.dot(
                    ref["weights"][row_tap, col_tap, channels],
                    cells_x[col_tap, :, first * LANES : (first + count) * LANES],
                    preferred_element_type=F32,
                )
                total = term if total is None else total + term
        for at in range(count):
            piece = total[:, at * LANES : (at + 1) * LANES]
            if "upstream" in ref:
                piece = piece + ref["upstream"][start + at].astype(F32)
            ref["out"][place] = piece.astype(ref["out"].dtype)
            place += 1
        block += count + 2


def finish_kernel(taps, scale, names, *refs):
    ref = dict(zip(names, refs))
    core = lax.axis_index("rep")
    halves = ref["out"].shape[2] // 2
    own = pl.multiple_of(core * halves, halves)
    other = pl.multiple_of((1 - core) * halves, halves)
    for tap in taps:
        @pl.when(pl.program_id(0) == tap - taps[0])
        def _():
            for col_tap in range(3):
                for who, where in (("mine", own), ("other", other)):
                    at = col_tap * halves
                    if tap == 2:
                        low = ref[f"{who}2"].shape[0]
                        for lo in range(0, halves, 16):
                            pos = at + lo
                            name, pos = (f"{who}2", pos) if pos < low else (f"{who}3", pos - low)
                            ref["out"][0, col_tap, pl.ds(pl.multiple_of(where + lo, 16), 16)] = (
                                ref[name][pos : pos + 16].astype(F32) * scale
                            )
                    else:
                        ref["out"][0, col_tap, pl.ds(where, halves)] = (
                            ref[f"{who}{tap}"][at : at + halves].astype(F32) * scale
                        )
    if "bias" in ref:
        local = ref["bias"].shape[1]
        ref["bias"][...] = ref["mine0"][3 * halves :, :local].astype(F32) * scale


def params(bytes_limit=VMEM_BYTES):
    return pltpu.CompilerParams(vmem_limit_bytes=bytes_limit)


def whole_spec(array):
    zeros = (0,) * array.ndim
    return pl.BlockSpec(array.shape, lambda *_: zeros)


def call(body, inputs, outputs, scratch, grid=(1,), specs=None, out_specs=None, aliases=None, flops=0):
    names = list(inputs) + list(outputs) + list(scratch)
    specs, out_specs = specs or {}, out_specs or {}
    shapes = {key: jax.ShapeDtypeStruct(*value) for key, value in outputs.items()}
    got = pl.pallas_call(
        functools.partial(body, names),
        grid=grid,
        in_specs=[specs.get(key) or whole_spec(value) for key, value in inputs.items()],
        out_specs=[out_specs.get(key) or whole_spec(value) for key, value in shapes.items()],
        out_shape=list(shapes.values()),
        scratch_shapes=[pltpu.VMEM(*value) for value in scratch.values()],
        input_output_aliases=aliases or {},
        compiler_params=params(),
        cost_estimate=pl.CostEstimate(flops=flops, bytes_accessed=4 * 2**20, transcendentals=0),
    )(*inputs.values())
    return dict(zip(shapes, got))


def per_device(features, kernel, shift_bias, upstream):
    rows, local, cols = upstream.shape
    groups = lax.axis_size("filt")
    chans = kernel.shape[3]
    halves = local // 2
    turns = range(1, groups)
    third = (rows - 1) // 3
    cuts = (third, 2 * third, rows - 1)

    def gather(cells):
        return {t: lax.ppermute(cells, "filt", shift_perm(groups, -t)) for t in turns}

    got = {"a": gather(features[: cuts[0]])}
    edge = call(
        lambda names, *refs: edge_kernel(*refs),
        {"cells": features},
        {"edge": ((local, LANES), BF16)},
        {},
    )["edge"]
    edge = swap_rep(edge)
    got["b"] = gather(jnp.concatenate([features[cuts[0] : cuts[1]], edge[None]], axis=0))
    down, up, down_perm, up_perm = send_rows(features, edge)
    above = lax.ppermute(down, "space", down_perm)
    below = lax.ppermute(up, "space", up_perm)
    got["c"] = gather(features[cuts[1] : cuts[2]])
    rim = jnp.concatenate(
        [features[cuts[2] :], below[:1], above[:1], below[1:], above[1:]], axis=0
    )
    got["d"] = gather(rim)
    weights_t = jnp.swapaxes(kernel, 2, 3)
    bias_wide = jnp.broadcast_to(shift_bias[:, None], (local, LANES))

    sets = [
        ("ab", [(1, cuts[1] - 2)]),
        ("bc", [(cuts[1] - 1, rows - 1 - cuts[1])]),
        ("abcd", [(rows - 2, 2), (0, 1)]),
    ]
    outs, slopes, held = [], [], []
    carried = {}
    for at, (parts, runs) in enumerate(sets):
        last = at == 2
        count = sum(n for _, n in runs)
        blocks = sum(n + 2 for _, n in runs)
        inputs = {
            "kernel": kernel,
            "bias": bias_wide,
            "features": features,
            "upstream": upstream,
            "edge": edge,
        }
        if last:
            inputs["above"], inputs["below"] = above, below
        for part in parts:
            for t in turns:
                inputs[f"{part}{t}"] = got[part][t]
        inputs.update(carried)
        specs = {"sum_in": pl.BlockSpec((1, 3, local, chans), lambda i: (i, 0, 0, 0))}
        outputs = {
            "block_out": ((count, local, cols), BF16),
            "slope": ((count, local, cols), BF16),
            "edge_out": ((local, LANES), BF16),
        }
        scratch = {
            "cells": ((3, chans, blocks * LANES), BF16),
            "slope_all": ((local, count * LANES), BF16),
        }
        aliases = {}
        if last:
            for tap in range(3):
                height = 3 * halves + (16 if tap == 0 else 0)
                outputs[f"away{tap}"] = ((height, chans), BF16)
                outputs[f"keep{tap}"] = ((height, chans), F32)
            scratch["hold"] = ((local, chans), F32)
        else:
            outputs["bias_out"] = ((16, local), F32)
            outputs["sum_out"] = ((3, 3, local, chans), F32)
            if at:
                aliases = {list(inputs).index("sum_in"): list(outputs).index("sum_out")}
        done = call(
            functools.partial(forward_kernel, runs, rows, cuts, groups, at > 0, last),
            inputs,
            outputs,
            scratch,
            grid=(3,),
            specs=specs,
            out_specs={"sum_out": pl.BlockSpec((1, 3, local, chans), lambda i: (i, 0, 0, 0))},
            aliases=aliases,
            flops=36 * local * chans * count * cols,
        )
        outs.append(done["block_out"])
        slopes.append(done["slope"])
        held.append([s + i for s, n in runs for i in range(n)])
        if not last:
            carried = {
                "edge_in": done["edge_out"],
                "bias_in": done["bias_out"],
                "sum_in": done["sum_out"],
            }
    block_out = jnp.concatenate([outs[2][2:], outs[0], outs[1], outs[2][:2]], axis=0)

    space = lax.axis_size("space")
    spot = lax.axis_index("space")
    low, high = space // 2 - 1, space // 2
    chunks = []
    for tap in range(3):
        came = swap_rep(done[f"away{tap}"])
        both = (done[f"keep{tap}"] + came.astype(F32)).astype(BF16)
        if tap == 2:
            cut = both.shape[0] // 2
            chunks += [both[:cut], both[cut:]]
        else:
            chunks.append(both)
    finals, others = [], []
    for part in chunks:
        for step in range(low):
            came = lax.ppermute(
                part, "space", [(step, step + 1), (space - 1 - step, space - 2 - step)]
            )
            part = (part.astype(F32) + came.astype(F32)).astype(BF16)
        came = lax.ppermute(part, "space", [(low, high), (high, low)])
        part = (part.astype(F32) + came.astype(F32)).astype(BF16)
        for step in reversed(range(low)):
            came = lax.ppermute(
                part, "space", [(step + 1, step), (space - 2 - step, space - 1 - step)]
            )
            part = jnp.where((spot == step) | (spot == space - 1 - step), came, part)
        finals.append(part)
        others.append(swap_rep(part))

    s_edge = swap_rep(done["edge_out"])
    s_first, s_last = slopes[2][2:], slopes[2][1:2]
    s_down = jnp.concatenate([s_last, s_edge[None]], axis=0)
    s_up = jnp.concatenate([s_first, s_edge[None]], axis=0)
    s_above = lax.ppermute(s_down, "space", down_perm)
    s_below = lax.ppermute(s_up, "space", up_perm)

    def backward(turn, runs, dtype):
        count = sum(n for _, n in runs)
        blocks = sum(n + 2 for _, n in runs)
        inputs = {"weights": weights_t, "edge": s_edge}
        for at, piece in enumerate(slopes):
            inputs[f"slope{at}"] = piece
        if any(s == 0 or s + n == rows for s, n in runs):
            inputs["above"], inputs["below"] = s_above, s_below
        if turn == 0:
            inputs["upstream"] = upstream
        return call(
            functools.partial(backward_kernel, runs, held, rows, turn, groups),
            inputs,
            {"out": ((count, local, cols), dtype)},
            {"cells": ((3, local, blocks * LANES), BF16)},
            flops=18 * local * local * count * cols,
        )["out"]

    mid = rows // 2
    pieces = [[(1, mid - 1)], [(mid, rows - 1 - mid)], [(0, 1), (rows - 1, 1)]]
    came = []
    for runs in pieces:
        arrived = []
        for t in turns:
            away = backward(t, runs, BF16)
            arrived.append(lax.ppermute(away, "filt", shift_perm(groups, t)))
        came.append(arrived)
    own = backward(0, [(0, rows)], F32)
    total = own
    for at in range(groups - 1):
        ends = came[2][at]
        whole = jnp.concatenate([ends[:1], came[0][at], came[1][at], ends[1:]], axis=0)
        total = total + whole.astype(F32)
    input_grad = total.astype(BF16)

    total_cells = rows * cols * space * lax.axis_size("rep")
    scale = 1.0 / float(total_cells) ** 0.5
    inputs = {"mine0": finals[0], "other0": others[0], "mine1": finals[1], "other1": others[1]}
    out_shape = ((3, 3, local, chans), F32)
    first = call(
        functools.partial(finish_kernel, (0, 1), scale),
        inputs,
        {"out": out_shape, "bias": ((16, local), F32)},
        {},
        grid=(2,),
        out_specs={"out": pl.BlockSpec((1, 3, local, chans), lambda i: (i, 0, 0, 0))},
    )
    inputs = {
        "mine2": finals[2], "mine3": finals[3], "other2": others[2], "other3": others[3],
        "before": first["out"],
    }
    kernel_grad = call(
        functools.partial(finish_kernel, (2,), scale),
        inputs,
        {"out": out_shape},
        {},
        specs={"before": pl.BlockSpec(memory_space=pl.ANY)},
        out_specs={"out": pl.BlockSpec((1, 3, local, chans), lambda i: (2, 0, 0, 0))},
        aliases={4: 0},
    )["out"]
    return block_out, input_grad, kernel_grad, first["bias"][0]


def solution(mesh):
    in_specs = (
        P(("parts", "space"), "filt", "rep"),
        P(None, None, "filt", None),
        P("filt"),
        P(("parts", "space"), "filt", "rep"),
    )
    out_specs = (
        P(("parts", "space"), "filt", "rep"),
        P(("parts", "space"), "filt", "rep"),
        P("parts", None, "filt", None),
        P(("parts", "filt")),
    )

    return jax.shard_map(
        per_device, mesh=mesh, in_specs=in_specs, out_specs=out_specs, check_vma=False
    )
```

time: 251 us -> 169 us (0.67)
  blocking collectives: 58.5 us -> 0 us
  waiting for transfers between devices: 103 us -> 67 us
  Pallas kernels: 0 us -> 34.7 us
  matrix products: 26.5 us -> 0 us
  starting transfers between devices: 21.7 us -> 44 us
  between operations: 14.2 us -> 1.16 us
  other arithmetic: 12.8 us -> 5.23 us
    all_gather x2 -> x0, waiting for transfers between devices: 73.7 us -> none  [the longest x1 39.7 us: per_device(): all_panels = lax.all_gather(rimmed, 'filt', axis=1, tiled=True)]
    ppermute x8 -> x32, waiting for transfers between devices: 6.85 us -> 67 us  [the longest x4 34.6 us: per_device(): lax.ppermute(part, 'space', [(step + 1, step), (space - 2 - step, space -...]
    all_to_all x1 -> x0, blocking collectives: 40.8 us -> none  [per_device(): lax.all_to_all(kernel, 'filt', split_axis=3, concat_axis=2, tiled=True)]
    pallas_call x0 -> x10, Pallas kernels: none -> 34.7 us  [call(): pl.pallas_call(functools.partial(body, names), grid=grid, in_specs=[specs...]
    dot_general x27 -> x0, matrix products: 26.5 us -> none  [the longest x9 11.2 us: forward_taps(): jnp.einsum('oc,hcw->how', weights, window, preferred_element_type=jnp.flo...]
    psum x1 -> x0, waiting for transfers between devices: 22.5 us -> none  [per_device(): kernel_sum, bias_sum = lax.psum((kernel_part, bias_part), ('space', 'rep'))]
    ppermute x8 -> x32, starting transfers between devices: 21.6 us -> 44 us  [the longest x4 11.6 us: per_device(): lax.ppermute(part, 'space', [(step, step + 1), (space - 1 - step, space -...]
    psum x1 -> x0, blocking collectives: 17.7 us -> none  [per_device(): kernel_sum, bias_sum = lax.psum((kernel_part, bias_part), ('space', 'rep'))]
  transfers between devices with their start and end apart: 11 -> 32, of which waited for: 9 -> 12; matrix products, arithmetic and copies ran while one was open for 7% -> 8% of each run, Pallas kernels for 0% -> 15%
where the time goes in v1:
time: 169 us; the launch traced here: 168 us
  waiting for transfers between devices  67 us (40%)
  starting transfers between devices  44 us (26%)
  Pallas kernels  34.7 us (21%)
  local copies, waits for them, and re-layouts  15.8 us (9%)
  other arithmetic  5.23 us (3%)
    pallas_call x10, Pallas kernels, call(): pl.pallas_call(functools.partial(body, names), grid=grid, in_specs=[specs...  34.7 us
    ppermute x4, waiting for transfers between devices, per_device(): lax.ppermute(part, 'space', [(step + 1, step), (space - 2 - step, space -...  34.6 us
    ppermute x4, waiting for transfers between devices, per_device(): lax.ppermute(part, 'space', [(step, step + 1), (space - 1 - step, space -...  14.2 us
    unnamed x21, local copies, waits for them, and re-layouts  13.5 us
    ppermute x4, starting transfers between devices, per_device(): lax.ppermute(part, 'space', [(step, step + 1), (space - 1 - step, space -...  11.6 us
    ppermute x4, waiting for transfers between devices, gather(): lax.ppermute(cells, 'filt', shift_perm(groups, -t))  7.98 us
    ppermute x3, waiting for transfers between devices, per_device(): arrived.append(lax.ppermute(away, 'filt', shift_perm(groups, t)))  6.8 us
    ppermute x3, starting transfers between devices, per_device(): arrived.append(lax.ppermute(away, 'filt', shift_perm(groups, t)))  5.45 us
  transfers between devices with their start and end apart: 32, of which 12 were waited for; matrix products, arithmetic and copies ran while one was open for 8% of the time, Pallas kernels for 15%

profile of v1, /device:TPU:0, one launch (start us, length us, event | category | flops | bytes accessed | tf_op | source)
XLA Modules:
  0.0 167.8 jit_solution(13622637681790050662)
XLA Ops:
  0.6 1.2 copy-done
  1.9 0.6 shard_map.75
  2.5 0.6 collective-permute-start
  3.0 0.7 constant_dynamic-update-slice_fusion
  3.7 0.3 collective-permute-done.refs_4_
  3.9 0.7 pad_maximum_fusion.2
  4.7 1.3 collective-permute-start.2
  6.0 1.0 fusion
  6.9 2.8 %collective-permute-start.3 = (bf16[5,256,128]{2,1,0:T(8,128)(2,1)}, bf16[5,256,128]{2,1,0:T(8,128)(2,1)}, u32[]{:S(2)}, u32[]{:S(2)}) collective-permute-start(bf16[5,256,128]{2,1,0:T(8,128)(2,1)} %get-tuple-element.51), channel_id=1, source_target_pairs={{0,2},{2,0},{1,3},{3,1},{4,6},{6,4},{5,7},{7,5},{8,10},{10,8},{9,1... | collective-permute-start | bytes 983048 | tf_op jit(solution)/shard_map/ppermute | solution.py:296
  9.8 2.9 %copy.10 = bf16[3,3,256,512]{2,3,1,0:T(8,128)(2,1)S(1)} copy(bf16[3,3,256,512]{3,2,1,0:T(8,128)(2,1)} %refs_0_.7) | data formatting | bytes 4718592 | tf_op args[1]
  12.7 1.0 pad_maximum_fusion.1
  13.7 2.1 %collective-permute-start.4 = (bf16[6,256,128]{2,1,0:T(8,128)(2,1)S(1)}, bf16[6,256,128]{2,1,0:T(8,128)(2,1)S(1)}, u32[]{:S(2)}, u32[]{:S(2)}) collective-permute-start(bf16[6,256,128]{2,1,0:T(8,128)(2,1)S(1)} %pad_maximum_fusion.1), channel_id=1, source_target_pairs={{0,2},{2,0},{1,3},{3,1},{4,6},{6,4},{5,7},{7,5},{8,10},{10,8},{9,1... | collective-permute-start | bytes 1179656 | tf_op jit(solution)/shard_map/ppermute | solution.py:296
  15.8 4.5 %collective-permute-start.1 = (bf16[2,256,128]{2,1,0:T(8,128)(2,1)}, bf16[2,256,128]{2,1,0:T(8,128)(2,1)S(1)}, u32[]{:S(2)}, u32[]{:S(2)}) collective-permute-start(bf16[2,256,128]{2,1,0:T(8,128)(2,1)} %get-tuple-element.63), channel_id=1, source_target_pairs={{0,4},{4,8},{8,12},{1,5},{5,9},{9,13},{2,6},{6,10},{10,14},{3,7},{... | collective-permute-start | bytes 393224 | tf_op jit(solution)/shard_map/ppermute | solution.py:308
  20.4 1.5 slice_dynamic-update-slice_fusion.3
  21.8 1.3 collective-permute-done.1.refs_5_
  23.2 0.6 slice_dynamic-update-slice_fusion.2
  23.8 1.5 slice_dynamic-update-slice_fusion.1
  25.3 0.6 slice_dynamic-update-slice_fusion
  26.0 8.0 %collective-permute-done.4.refs_6_.refs_5_.refs_8_ = bf16[6,256,128]{2,1,0:T(8,128)(2,1)S(1)} collective-permute-done((bf16[6,256,128]{2,1,0:T(8,128)(2,1)S(1)}, bf16[6,256,128]{2,1,0:T(8,128)(2,1)S(1)}, u32[]{:S(2)}, u32[]{:S(2)}) %collective-permute-start.4) | collective-permute-done | bytes 393248 | tf_op jit(solution)/shard_map/ppermute | solution.py:296
  34.1 1.7 copy-done.2
  35.8 1.2 copy-done.5
  37.0 8.8 %shard_map.76 = (bf16[8,256,128]{2,1,0:T(8,128)(2,1)S(1)}, bf16[8,256,128]{2,1,0:T(8,128)(2,1)S(1)}, bf16[256,128]{1,0:T(8,128)(2,1)S(1)}, f32[16,256]{1,0:T(8,128)S(1)}, f32[3,3,256,512]{3,2,1,0:T(8,128)S(1)}) custom-call(bf16[3,3,256,512]{3,2,1,0:T(8,128)(2,1)S(1)} %copy-done.2, f32[256,128]{1,0:T(8,128)S(1)} %broadcast_in_dim.6.refs_1_, ...), custom_call_target="tpu_custom_call" | custom-call | flops 4831838208 | bytes 4194304 | tf_op jit(solution)/shard_map/pallas_call | solution.py:272
  45.8 7.1 %shard_map.77 = (bf16[5,256,128]{2,1,0:T(8,128)(2,1)S(1)}, bf16[5,256,128]{2,1,0:T(8,128)(2,1)S(1)}, bf16[256,128]{1,0:T(8,128)(2,1)S(1)}, f32[16,256]{1,0:T(8,128)S(1)}, f32[3,3,256,512]{3,2,1,0:T(8,128)S(1)}) custom-call(bf16[3,3,256,512]{3,2,1,0:T(8,128)(2,1)S(1)} %copy-done.2, ...), custom_call_target="tpu_custom_call", output_to_operand_aliasing={{4}: (9, {})} | custom-call | flops 3019898880 | bytes 4194304 | tf_op jit(solution)/shard_map/pallas_call | solution.py:272
  52.9 2.2 %copy-done.4 = f32[3,3,256,512]{3,2,1,0:T(8,128)} copy-done((f32[3,3,256,512]{3,2,1,0:T(8,128)}, f32[3,3,256,512]{3,2,1,0:T(8,128)S(1)}, u32[]{:S(2)}) %copy-start.4) | copy-done | bytes 4718616
  55.1 7.7 %shard_map.78 = (bf16[3,256,128]{2,1,0:T(8,128)(2,1)S(1)}, bf16[3,256,128]{2,1,0:T(8,128)(2,1)S(1)}, bf16[256,128]{1,0:T(8,128)(2,1)S(1)}, bf16[400,512]{1,0:T(8...) custom-call(bf16[3,3,256,512]{3,2,1,0:T(8,128)(2,1)S(1)} %copy-done., ...), custom_call_target="tpu_custom_call" | custom-call | flops 1811939328 | bytes 4194304 | tf_op jit(solution)/shard_map/pallas_call | solution.py:272
  62.9 0.5 collective-permute-start.22
  63.5 0.4 collective-permute-start.7
  63.9 1.1 pad_maximum_fusion
  65.0 0.8 collective-permute-done.7.refs_1_
  65.9 4.7 %collective-permute-start.8 = (bf16[2,256,128]{2,1,0:T(8,128)(2,1)S(1)}, bf16[2,256,128]{2,1,0:T(8,128)(2,1)S(1)}, u32[]{:S(2)}, u32[]{:S(2)}) collective-permute-start(bf16[2,256,128]{2,1,0:T(8,128)(2,1)S(1)} %get-tuple-element.61), channel_id=1, source_target_pairs={{0,4},{4,8},{8,12},{1,5},{5,9},{9,13},{2,6},{6,10},{10,14},{3,7},{... | collective-permute-start | bytes 393224 | tf_op jit(solution)/shard_map/ppermute | solution.py:419
  70.5 1.3 collective-permute-start.9
  71.8 1.7 %shard_map.81 = bf16[7,256,128]{2,1,0:T(8,128)(2,1)S(1)} custom-call(bf16[3,3,512,256]{3,2,1,0:T(8,128)(2,1)S(1)} %bitcast.4, bf16[256,128]{1,0:T(8,128)(2,1)S(1)} %collective-permute-done.7.refs_1_, bf16[8,256,128]{2,1,0:T(8,128)(2,1)S(1)} %get-tuple-element.35.refs_2_, bf16[5,256,128]{2,1,0:T(8,128)(2,1)S(1)} %get-tuple-element.36.refs_3_, ...), custom_call_target="tpu_custom_call" | custom-call | flops 1056964608 | bytes 4194304 | tf_op jit(solution)/shard_map/pallas_call | solution.py:272
  73.5 1.7 %shard_map.82 = bf16[7,256,128]{2,1,0:T(8,128)(2,1)S(1)} custom-call(bf16[3,3,512,256]{3,2,1,0:T(8,128)(2,1)S(1)} %bitcast.5, bf16[256,128]{1,0:T(8,128)(2,1)S(1)} %collective-permute-done.7.refs_1_, bf16[8,256,128]{2,1,0:T(8,128)(2,1)S(1)} %get-tuple-element.35.refs_2_, bf16[5,256,128]{2,1,0:T(8,128)(2,1)S(1)} %get-tuple-element.36.refs_3_, ...), custom_call_target="tpu_custom_call" | custom-call | flops 1056964608 | bytes 4194304 | tf_op jit(solution)/shard_map/pallas_call | solution.py:272
  75.2 2.0 %collective-permute-start.11 = (bf16[7,256,128]{2,1,0:T(8,128)(2,1)S(1)}, bf16[7,256,128]{2,1,0:T(8,128)(2,1)S(1)}, u32[]{:S(2)}, u32[]{:S(2)}) collective-permute-start(bf16[7,256,128]{2,1,0:T(8,128)(2,1)S(1)} %shard_map.81), channel_id=1, source_target_pairs={{0,2},{2,0},{1,3},{3,1},{4,6},{6,4},{5,7},{7,5},{8,10},{10,8},{9,1... | collective-permute-start | bytes 1376264 | tf_op jit(solution)/shard_map/ppermute | solution.py:447
  77.2 0.7 collective-permute-done.9.refs_6_
  78.0 0.9 shard_map.80
  78.9 1.7 %collective-permute-start.10 = (bf16[2,256,128]{2,1,0:T(8,128)(2,1)S(1)}, bf16[2,256,128]{2,1,0:T(8,128)(2,1)S(1)}, u32[]{:S(2)}, u32[]{:S(2)}) collective-permute-start(bf16[2,256,128]{2,1,0:T(8,128)(2,1)S(1)} %shard_map.80), channel_id=1, source_target_pairs={{0,2},{2,0},{1,3},{3,1},{4,6},{6,4},{5,7},{7,5},{8,10},{10,8},{9,1... | collective-permute-start | bytes 393224 | tf_op jit(solution)/shard_map/ppermute | solution.py:447
  80.6 3.2 %shard_map.79 = f32[16,256,128]{2,1,0:T(8,128)S(1)} custom-call(bf16[3,3,512,256]{3,2,1,0:T(8,128)(2,1)S(1)} %bitcast.7, bf16[256,128]{1,0:T(8,128)(2,1)S(1)} %collective-permute-done.7.refs_1_, bf16[8,256,128]{2,1,0:T(8,128)(2,1)S(1)} %get-tuple-element.35.refs_2_, bf16[5,256,128]{2,1,0:T(8,128)(2,1)S(1)} %get-tuple-element.36.refs_3_, ...), custom_call_target="tpu_custom_call" | custom-call | flops 2415919104 | bytes 4194304 | tf_op jit(solution)/shard_map/pallas_call | solution.py:272
  83.8 6.8 %collective-permute-done.10 = bf16[2,256,128]{2,1,0:T(8,128)(2,1)S(1)} collective-permute-done((bf16[2,256,128]{2,1,0:T(8,128)(2,1)S(1)}, bf16[2,256,128]{2,1,0:T(8,128)(2,1)S(1)}, u32[]{:S(2)}, u32[]{:S(2)}) %collective-permute-start.10) | collective-permute-done | bytes 131104 | tf_op jit(solution)/shard_map/ppermute | solution.py:447
  90.6 1.7 %collective-permute-start.12 = (bf16[7,256,128]{2,1,0:T(8,128)(2,1)S(1)}, bf16[7,256,128]{2,1,0:T(8,128)(2,1)S(1)}, u32[]{:S(2)}, u32[]{:S(2)}) collective-permute-start(bf16[7,256,128]{2,1,0:T(8,128)(2,1)S(1)} %shard_map.82), channel_id=1, source_target_pairs={{0,2},{2,0},{1,3},{3,1},{4,6},{6,4},{5,7},{7,5},{8,10},{10,8},{9,1... | collective-permute-start | bytes 1376264 | tf_op jit(solution)/shard_map/ppermute | solution.py:447
  92.5 4.3 %collective-permute-start.28 = (bf16[384,512]{1,0:T(8,128)(2,1)S(1)}, bf16[384,512]{1,0:T(8,128)(2,1)S(1)}, u32[]{:S(2)}, u32[]{:S(2)}) collective-permute-start(bf16[384,512]{1,0:T(8,128)(2,1)S(1)} %add_convert_fusion.6), channel_id=1, source_target_pairs={{0,4},{12,8},{1,5},{13,9},{2,6},{14,10},{3,7},{15,11},{16,20},{28,... | collective-permute-start | bytes 1179656 | tf_op jit(solution)/shard_map/ppermute | solution.py:401
  97.0 1.5 collective-permute-start.14
  98.5 1.3 collective-permute-start.17
  99.8 0.1 add_convert_fusion.3
  99.9 10.1 %collective-permute-done.14 = bf16[192,512]{1,0:T(8,128)(2,1)S(1)} collective-permute-done((bf16[192,512]{1,0:T(8,128)(2,1)S(1)}, bf16[192,512]{1,0:T(8,128)(2,1)S(1)}, u32[]{:S(2)}, u32[]{:S(2)}) %collective-permute-start.14) | collective-permute-done | bytes 196640 | tf_op jit(solution)/shard_map/ppermute | solution.py:401
  110.0 4.4 %collective-permute-start.23 = (bf16[400,512]{1,0:T(8,128)(2,1)S(1)}, bf16[400,512]{1,0:T(8,128)(2,1)S(1)}, u32[]{:S(2)}, u32[]{:S(2)}) collective-permute-start(bf16[400,512]{1,0:T(8,128)(2,1)S(1)} %add_convert_fusion.3), channel_id=1, source_target_pairs={{0,4},{12,8},{1,5},{13,9},{2,6},{14,10},{3,7},{15,11},{16,20},{28,... | collective-permute-start | bytes 1228808 | tf_op jit(solution)/shard_map/ppermute | solution.py:401
  114.6 0.7 collective-permute-start.18
  115.3 0.7 collective-permute-start.15
  116.1 0.7 collective-permute-start.29
  116.8 4.1 %collective-permute-done.23 = bf16[400,512]{1,0:T(8,128)(2,1)S(1)} collective-permute-done((bf16[400,512]{1,0:T(8,128)(2,1)S(1)}, bf16[400,512]{1,0:T(8,128)(2,1)S(1)}, u32[]{:S(2)}, u32[]{:S(2)}) %collective-permute-start.23) | collective-permute-done | bytes 409632 | tf_op jit(solution)/shard_map/ppermute | solution.py:401
  120.9 1.3 collective-permute-start.19
  122.3 0.7 collective-permute-start.24
  123.1 1.3 collective-permute-start.16
  124.5 1.3 collective-permute-start.30
  125.9 8.1 %collective-permute-done.19 = bf16[192,512]{1,0:T(8,128)(2,1)S(1)} collective-permute-done((bf16[192,512]{1,0:T(8,128)(2,1)S(1)}, bf16[192,512]{1,0:T(8,128)(2,1)S(1)}, u32[]{:S(2)}, u32[]{:S(2)}) %collective-permute-start.19) | collective-permute-done | bytes 196640 | tf_op jit(solution)/shard_map/ppermute | solution.py:408
  134.1 1.3 collective-permute-start.25
  135.4 20.4 %collective-permute-done.30 = bf16[384,512]{1,0:T(8,128)(2,1)S(1)} collective-permute-done((bf16[384,512]{1,0:T(8,128)(2,1)S(1)}, bf16[384,512]{1,0:T(8,128)(2,1)S(1)}, u32[]{:S(2)}, u32[]{:S(2)}) %collective-permute-start.30) | collective-permute-done | bytes 393248 | tf_op jit(solution)/shard_map/ppermute | solution.py:408
  155.9 6.0 %collective-permute-done.25 = bf16[400,512]{1,0:T(8,128)(2,1)S(1)} collective-permute-done((bf16[400,512]{1,0:T(8,128)(2,1)S(1)}, bf16[400,512]{1,0:T(8,128)(2,1)S(1)}, u32[]{:S(2)}, u32[]{:S(2)}) %collective-permute-start.25) | collective-permute-done | bytes 409632 | tf_op jit(solution)/shard_map/ppermute | solution.py:408
  162.0 0.6 collective-permute-start.26
  162.7 1.2 add_convert_fusion
  163.9 0.3 collective-permute-done.26.refs_1_
  164.2 1.8 %shard_map.83 = (f32[3,3,256,512]{3,2,1,0:T(8,128)}, f32[16,256]{1,0:T(8,128)S(1)}) custom-call(bf16[400,512]{1,0:T(8,128)(2,1)S(1)} %broadcast_select_fusion.refs_0_, bf16[400,512]{1,0:T(8,128)(2,1)S(1)} %collective-permute-done.26.refs_1_, bf16[384,512]{1,0:T(8,128)(2,1)S(1)} %broadcast_select_fusion.1.refs_2_, ...), custom_call_target="tpu_custom_call" | custom-call | bytes 4194304 | tf_op jit(solution)/shard_map/pallas_call | solution.py:272
  166.0 0.6 slice.72
  166.5 1.3 shard_map.84
  (59 shorter events, 1.6 us)
Async XLA Ops:
  0.6 1.2 copy-start
  2.5 1.5 collective-permute-start
  4.7 15.7 %collective-permute-start.2 = (bf16[2,256,128]{2,1,0:T(8,128)(2,1)}, bf16[2,256,128]{2,1,0:T(8,128)(2,1)}, u32[]{:S(2)}, u32[]{:S(2)}) collective-permute-start(bf16[2,256,128]{2,1,0:T(8,128)(2,1)} %get-tuple-element.62), channel_id=1, source_target_pairs={{4,0},{8,4},{12,8},{5,1},{9,5},{13,9},{6,2},{10,6},{14,10},{7,3},{... | collective-permute-start | bytes 393224 | tf_op jit(solution)/shard_map/ppermute | solution.py:309
  6.9 19.1 %collective-permute-start.3 = (bf16[5,256,128]{2,1,0:T(8,128)(2,1)}, bf16[5,256,128]{2,1,0:T(8,128)(2,1)}, u32[]{:S(2)}, u32[]{:S(2)}) collective-permute-start(bf16[5,256,128]{2,1,0:T(8,128)(2,1)} %get-tuple-element.51), channel_id=1, source_target_pairs={{0,2},{2,0},{1,3},{3,1},{4,6},{6,4},{5,7},{7,5},{8,10},{10,8},{9,1... | collective-permute-start | bytes 983048 | tf_op jit(solution)/shard_map/ppermute | solution.py:296
  9.8 36.0 %collective-permute-start.5 = (bf16[5,256,128]{2,1,0:T(8,128)(2,1)}, bf16[5,256,128]{2,1,0:T(8,128)(2,1)}, u32[]{:S(2)}, u32[]{:S(2)}) collective-permute-start(bf16[5,256,128]{2,1,0:T(8,128)(2,1)} %get-tuple-element.49), channel_id=1, source_target_pairs={{0,2},{2,0},{1,3},{3,1},{4,6},{6,4},{5,7},{7,5},{8,10},{10,8},{9,1... | collective-permute-start | bytes 983048 | tf_op jit(solution)/shard_map/ppermute | solution.py:296
  9.8 24.2 %copy-start.7 = (f32[256]{0:T(256)S(1)}, f32[256]{0:T(256)}, u32[]{:S(2)}) copy-start(f32[256]{0:T(256)} %param.6) | copy-start | bytes 3076
  9.8 24.3 %copy-start.1 = (bf16[16,256,128]{2,1,0:T(8,128)(2,1)S(1)}, bf16[16,256,128]{2,1,0:T(8,128)(2,1)}, u32[]{:S(2)}) copy-start(bf16[16,256,128]{2,1,0:T(8,128)(2,1)} %refs_2_.5) | copy-start | bytes 3145732
  13.7 20.2 %collective-permute-start.4 = (bf16[6,256,128]{2,1,0:T(8,128)(2,1)S(1)}, bf16[6,256,128]{2,1,0:T(8,128)(2,1)S(1)}, u32[]{:S(2)}, u32[]{:S(2)}) collective-permute-start(bf16[6,256,128]{2,1,0:T(8,128)(2,1)S(1)} %pad_maximum_fusion.1), channel_id=1, source_target_pairs={{0,2},{2,0},{1,3},{3,1},{4,6},{6,4},{5,7},{7,5},{8,10},{10,8},{9,1... | collective-permute-start | bytes 1179656 | tf_op jit(solution)/shard_map/ppermute | solution.py:296
  15.8 7.4 %collective-permute-start.1 = (bf16[2,256,128]{2,1,0:T(8,128)(2,1)}, bf16[2,256,128]{2,1,0:T(8,128)(2,1)S(1)}, u32[]{:S(2)}, u32[]{:S(2)}) collective-permute-start(bf16[2,256,128]{2,1,0:T(8,128)(2,1)} %get-tuple-element.63), channel_id=1, source_target_pairs={{0,4},{4,8},{8,12},{1,5},{5,9},{9,13},{2,6},{6,10},{10,14},{3,7},{... | collective-permute-start | bytes 393224 | tf_op jit(solution)/shard_map/ppermute | solution.py:308
  25.9 29.2 %collective-permute-start.6 = (bf16[5,256,128]{2,1,0:T(8,128)(2,1)}, bf16[5,256,128]{2,1,0:T(8,128)(2,1)S(1)}, u32[]{:S(2)}, u32[]{:S(2)}) collective-permute-start(bf16[5,256,128]{2,1,0:T(8,128)(2,1)} %slice_dynamic-update-slice_fusion), channel_id=1, source_target_pairs={{0,2},{2,0},{1,3},{3,1},{4,6},{6,4},{5,7},{7,5},{8,10},{10,8},{9,1... | collective-permute-start | bytes 983048 | tf_op jit(solution)/shard_map/ppermute | solution.py:296
  34.1 1.7 copy-start.2
  35.7 1.2 copy-start.5
  45.8 9.3 %copy-start.3 = (bf16[3,3,256,512]{3,2,1,0:T(8,128)(2,1)S(1)}, bf16[3,3,256,512]{3,2,1,0:T(8,128)(2,1)}, u32[]{:S(2)}) copy-start(bf16[3,3,256,512]{3,2,1,0:T(8,128)(2,1)} %refs_0_.7) | copy-start | bytes 7077892
  45.8 9.3 %copy-start.6 = (bf16[16,256,128]{2,1,0:T(8,128)(2,1)S(1)}, bf16[16,256,128]{2,1,0:T(8,128)(2,1)}, u32[]{:S(2)}) copy-start(bf16[16,256,128]{2,1,0:T(8,128)(2,1)} %refs_7_.1) | copy-start | bytes 3145732
  52.9 2.2 %copy-start.4 = (f32[3,3,256,512]{3,2,1,0:T(8,128)}, f32[3,3,256,512]{3,2,1,0:T(8,128)S(1)}, u32[]{:S(2)}) copy-start(f32[3,3,256,512]{3,2,1,0:T(8,128)S(1)} %get-tuple-element.30.refs_13_) | copy-start | bytes 14155780
  62.8 29.5 %collective-permute-start.27 = (bf16[384,512]{1,0:T(8,128)(2,1)S(1)}, bf16[384,512]{1,0:T(8,128)(2,1)S(1)}, u32[]{:S(2)}, u32[]{:S(2)}) collective-permute-start(bf16[384,512]{1,0:T(8,128)(2,1)S(1)} %get-tuple-element.43), channel_id=1, source_target_pairs={{0,1},{1,0},{2,3},{3,2},{4,5},{5,4},{6,7},{7,6},{8,9},{9,8},{10,11... | collective-permute-start | bytes 1179656 | tf_op jit(solution)/shard_map/ppermute | solution.py:21
  62.9 35.6 %collective-permute-start.22 = (bf16[400,512]{1,0:T(8,128)(2,1)S(1)}, bf16[400,512]{1,0:T(8,128)(2,1)S(1)}, u32[]{:S(2)}, u32[]{:S(2)}) collective-permute-start(bf16[400,512]{1,0:T(8,128)(2,1)S(1)} %get-tuple-element.41), channel_id=1, source_target_pairs={{0,1},{1,0},{2,3},{3,2},{4,5},{5,4},{6,7},{7,6},{8,9},{9,8},{10,11... | collective-permute-start | bytes 1228808 | tf_op jit(solution)/shard_map/ppermute | solution.py:21
  63.4 33.4 %collective-permute-start.13 = (bf16[384,512]{1,0:T(8,128)(2,1)S(1)}, bf16[384,512]{1,0:T(8,128)(2,1)S(1)}, u32[]{:S(2)}, u32[]{:S(2)}) collective-permute-start(bf16[384,512]{1,0:T(8,128)(2,1)S(1)} %get-tuple-element.39), channel_id=1, source_target_pairs={{0,1},{1,0},{2,3},{3,2},{4,5},{5,4},{6,7},{7,6},{8,9},{9,8},{10,11... | collective-permute-start | bytes 1179656 | tf_op jit(solution)/shard_map/ppermute | solution.py:21
  63.5 2.4 %collective-permute-start.7 = (bf16[256,128]{1,0:T(8,128)(2,1)S(1)}, bf16[256,128]{1,0:T(8,128)(2,1)S(1)}, u32[]{:S(2)}, u32[]{:S(2)}) collective-permute-start(bf16[256,128]{1,0:T(8,128)(2,1)S(1)} %get-tuple-element.34), channel_id=1, source_target_pairs={{0,1},{1,0},{2,3},{3,2},{4,5},{5,4},{6,7},{7,6},{8,9},{9,8},{10,11... | collective-permute-start | bytes 196616 | tf_op jit(solution)/shard_map/ppermute | solution.py:21
  65.9 9.4 %collective-permute-start.8 = (bf16[2,256,128]{2,1,0:T(8,128)(2,1)S(1)}, bf16[2,256,128]{2,1,0:T(8,128)(2,1)S(1)}, u32[]{:S(2)}, u32[]{:S(2)}) collective-permute-start(bf16[2,256,128]{2,1,0:T(8,128)(2,1)S(1)} %get-tuple-element.61), channel_id=1, source_target_pairs={{0,4},{4,8},{8,12},{1,5},{5,9},{9,13},{2,6},{6,10},{10,14},{3,7},{... | collective-permute-start | bytes 393224 | tf_op jit(solution)/shard_map/ppermute | solution.py:419
  70.5 7.4 %collective-permute-start.9 = (bf16[2,256,128]{2,1,0:T(8,128)(2,1)S(1)}, bf16[2,256,128]{2,1,0:T(8,128)(2,1)S(1)}, u32[]{:S(2)}, u32[]{:S(2)}) collective-permute-start(bf16[2,256,128]{2,1,0:T(8,128)(2,1)S(1)} %get-tuple-element.60), channel_id=1, source_target_pairs={{4,0},{8,4},{12,8},{5,1},{9,5},{13,9},{6,2},{10,6},{14,10},{7,3},{... | collective-permute-start | bytes 393224 | tf_op jit(solution)/shard_map/ppermute | solution.py:420
  75.2 87.3 %collective-permute-start.11 = (bf16[7,256,128]{2,1,0:T(8,128)(2,1)S(1)}, bf16[7,256,128]{2,1,0:T(8,128)(2,1)S(1)}, u32[]{:S(2)}, u32[]{:S(2)}) collective-permute-start(bf16[7,256,128]{2,1,0:T(8,128)(2,1)S(1)} %shard_map.81), channel_id=1, source_target_pairs={{0,2},{2,0},{1,3},{3,1},{4,6},{6,4},{5,7},{7,5},{8,10},{10,8},{9,1... | collective-permute-start | bytes 1376264 | tf_op jit(solution)/shard_map/ppermute | solution.py:447
  78.9 11.7 %collective-permute-start.10 = (bf16[2,256,128]{2,1,0:T(8,128)(2,1)S(1)}, bf16[2,256,128]{2,1,0:T(8,128)(2,1)S(1)}, u32[]{:S(2)}, u32[]{:S(2)}) collective-permute-start(bf16[2,256,128]{2,1,0:T(8,128)(2,1)S(1)} %shard_map.80), channel_id=1, source_target_pairs={{0,2},{2,0},{1,3},{3,1},{4,6},{6,4},{5,7},{7,5},{8,10},{10,8},{9,1... | collective-permute-start | bytes 393224 | tf_op jit(solution)/shard_map/ppermute | solution.py:447
  90.6 72.1 %collective-permute-start.12 = (bf16[7,256,128]{2,1,0:T(8,128)(2,1)S(1)}, bf16[7,256,128]{2,1,0:T(8,128)(2,1)S(1)}, u32[]{:S(2)}, u32[]{:S(2)}) collective-permute-start(bf16[7,256,128]{2,1,0:T(8,128)(2,1)S(1)} %shard_map.82), channel_id=1, source_target_pairs={{0,2},{2,0},{1,3},{3,1},{4,6},{6,4},{5,7},{7,5},{8,10},{10,8},{9,1... | collective-permute-start | bytes 1376264 | tf_op jit(solution)/shard_map/ppermute | solution.py:447
  92.5 22.8 %collective-permute-start.28 = (bf16[384,512]{1,0:T(8,128)(2,1)S(1)}, bf16[384,512]{1,0:T(8,128)(2,1)S(1)}, u32[]{:S(2)}, u32[]{:S(2)}) collective-permute-start(bf16[384,512]{1,0:T(8,128)(2,1)S(1)} %add_convert_fusion.6), channel_id=1, source_target_pairs={{0,4},{12,8},{1,5},{13,9},{2,6},{14,10},{3,7},{15,11},{16,20},{28,... | collective-permute-start | bytes 1179656 | tf_op jit(solution)/shard_map/ppermute | solution.py:401
  97.0 13.1 %collective-permute-start.14 = (bf16[192,512]{1,0:T(8,128)(2,1)S(1)}, bf16[192,512]{1,0:T(8,128)(2,1)S(1)}, u32[]{:S(2)}, u32[]{:S(2)}) collective-permute-start(bf16[192,512]{1,0:T(8,128)(2,1)S(1)} %get-tuple-element.55), channel_id=1, source_target_pairs={{0,4},{12,8},{1,5},{13,9},{2,6},{14,10},{3,7},{15,11},{16,20},{28,... | collective-permute-start | bytes 589832 | tf_op jit(solution)/shard_map/ppermute | solution.py:401
  98.5 16.0 %collective-permute-start.17 = (bf16[192,512]{1,0:T(8,128)(2,1)S(1)}, bf16[192,512]{1,0:T(8,128)(2,1)S(1)}, u32[]{:S(2)}, u32[]{:S(2)}) collective-permute-start(bf16[192,512]{1,0:T(8,128)(2,1)S(1)} %get-tuple-element.54), channel_id=1, source_target_pairs={{0,4},{12,8},{1,5},{13,9},{2,6},{14,10},{3,7},{15,11},{16,20},{28,... | collective-permute-start | bytes 589832 | tf_op jit(solution)/shard_map/ppermute | solution.py:401
  110.0 10.9 %collective-permute-start.23 = (bf16[400,512]{1,0:T(8,128)(2,1)S(1)}, bf16[400,512]{1,0:T(8,128)(2,1)S(1)}, u32[]{:S(2)}, u32[]{:S(2)}) collective-permute-start(bf16[400,512]{1,0:T(8,128)(2,1)S(1)} %add_convert_fusion.3), channel_id=1, source_target_pairs={{0,4},{12,8},{1,5},{13,9},{2,6},{14,10},{3,7},{15,11},{16,20},{28,... | collective-permute-start | bytes 1228808 | tf_op jit(solution)/shard_map/ppermute | solution.py:401
  114.6 1.5 collective-permute-start.18
  115.3 7.0 %collective-permute-start.15 = (bf16[192,512]{1,0:T(8,128)(2,1)S(1)}, bf16[192,512]{1,0:T(8,128)(2,1)S(1)}, u32[]{:S(2)}, u32[]{:S(2)}) collective-permute-start(bf16[192,512]{1,0:T(8,128)(2,1)S(1)} %get-tuple-element.53), channel_id=1, source_target_pairs={{4,8},{8,4},{5,9},{9,5},{6,10},{10,6},{7,11},{11,7},{20,24},{24,20... | collective-permute-start | bytes 589832 | tf_op jit(solution)/shard_map/ppermute | solution.py:405
  116.1 7.0 %collective-permute-start.29 = (bf16[384,512]{1,0:T(8,128)(2,1)S(1)}, bf16[384,512]{1,0:T(8,128)(2,1)S(1)}, u32[]{:S(2)}, u32[]{:S(2)}) collective-permute-start(bf16[384,512]{1,0:T(8,128)(2,1)S(1)} %add_convert_fusion.5), channel_id=1, source_target_pairs={{4,8},{8,4},{5,9},{9,5},{6,10},{10,6},{7,11},{11,7},{20,24},{24,20... | collective-permute-start | bytes 1179656 | tf_op jit(solution)/shard_map/ppermute | solution.py:405
  120.9 13.1 %collective-permute-start.19 = (bf16[192,512]{1,0:T(8,128)(2,1)S(1)}, bf16[192,512]{1,0:T(8,128)(2,1)S(1)}, u32[]{:S(2)}, u32[]{:S(2)}) collective-permute-start(bf16[192,512]{1,0:T(8,128)(2,1)S(1)} %add_convert_fusion.8), channel_id=1, source_target_pairs={{4,0},{8,12},{5,1},{9,13},{6,2},{10,14},{7,3},{11,15},{20,16},{24,... | collective-permute-start | bytes 589832 | tf_op jit(solution)/shard_map/ppermute | solution.py:408
  122.3 2.2 %collective-permute-start.24 = (bf16[400,512]{1,0:T(8,128)(2,1)S(1)}, bf16[400,512]{1,0:T(8,128)(2,1)S(1)}, u32[]{:S(2)}, u32[]{:S(2)}) collective-permute-start(bf16[400,512]{1,0:T(8,128)(2,1)S(1)} %add_convert_fusion.2), channel_id=1, source_target_pairs={{4,8},{8,4},{5,9},{9,5},{6,10},{10,6},{7,11},{11,7},{20,24},{24,20... | collective-permute-start | bytes 1228808 | tf_op jit(solution)/shard_map/ppermute | solution.py:405
  123.1 38.9 %collective-permute-start.16 = (bf16[192,512]{1,0:T(8,128)(2,1)S(1)}, bf16[192,512]{1,0:T(8,128)(2,1)S(1)}, u32[]{:S(2)}, u32[]{:S(2)}) collective-permute-start(bf16[192,512]{1,0:T(8,128)(2,1)S(1)} %add_convert_fusion.10), channel_id=1, source_target_pairs={{4,0},{8,12},{5,1},{9,13},{6,2},{10,14},{7,3},{11,15},{20,16},{24,... | collective-permute-start | bytes 589832 | tf_op jit(solution)/shard_map/ppermute | solution.py:408
  124.5 31.3 %collective-permute-start.30 = (bf16[384,512]{1,0:T(8,128)(2,1)S(1)}, bf16[384,512]{1,0:T(8,128)(2,1)S(1)}, u32[]{:S(2)}, u32[]{:S(2)}) collective-permute-start(bf16[384,512]{1,0:T(8,128)(2,1)S(1)} %add_convert_fusion.4), channel_id=1, source_target_pairs={{4,0},{8,12},{5,1},{9,13},{6,2},{10,14},{7,3},{11,15},{20,16},{24,... | collective-permute-start | bytes 1179656 | tf_op jit(solution)/shard_map/ppermute | solution.py:408
  134.1 27.8 %collective-permute-start.25 = (bf16[400,512]{1,0:T(8,128)(2,1)S(1)}, bf16[400,512]{1,0:T(8,128)(2,1)S(1)}, u32[]{:S(2)}, u32[]{:S(2)}) collective-permute-start(bf16[400,512]{1,0:T(8,128)(2,1)S(1)} %add_convert_fusion.1), channel_id=1, source_target_pairs={{4,0},{8,12},{5,1},{9,13},{6,2},{10,14},{7,3},{11,15},{20,16},{24,... | collective-permute-start | bytes 1228808 | tf_op jit(solution)/shard_map/ppermute | solution.py:408
  155.8 10.7 %collective-permute-start.21 = (bf16[192,512]{1,0:T(8,128)(2,1)S(1)}, bf16[192,512]{1,0:T(8,128)(2,1)S(1)}, u32[]{:S(2)}, u32[]{:S(2)}) collective-permute-start(bf16[192,512]{1,0:T(8,128)(2,1)S(1)} %broadcast_select_fusion.2.refs_1_), channel_id=1, source_target_pairs={{0,1},{1,0},{2,3},{3,2},{4,5},{5,4},{6,7},{7,6},{8,9},{9,8},{10,11... | collective-permute-start | bytes 589832 | tf_op jit(solution)/shard_map/ppermute | solution.py:21
  161.9 2.0 %collective-permute-start.31 = (bf16[384,512]{1,0:T(8,128)(2,1)S(1)}, bf16[384,512]{1,0:T(8,128)(2,1)S(1)}, u32[]{:S(2)}, u32[]{:S(2)}) collective-permute-start(bf16[384,512]{1,0:T(8,128)(2,1)S(1)} %broadcast_select_fusion.1.refs_2_), channel_id=1, source_target_pairs={{0,1},{1,0},{2,3},{3,2},{4,5},{5,4},{6,7},{7,6},{8,9},{9,8},{10,11... | collective-permute-start | bytes 1179656 | tf_op jit(solution)/shard_map/ppermute | solution.py:21
  162.0 2.2 %collective-permute-start.26 = (bf16[400,512]{1,0:T(8,128)(2,1)S(1)}, bf16[400,512]{1,0:T(8,128)(2,1)S(1)}, u32[]{:S(2)}, u32[]{:S(2)}) collective-permute-start(bf16[400,512]{1,0:T(8,128)(2,1)S(1)} %broadcast_select_fusion.refs_0_), channel_id=1, source_target_pairs={{0,1},{1,0},{2,3},{3,2},{4,5},{5,4},{6,7},{7,6},{8,9},{9,8},{10,11... | collective-permute-start | bytes 1228808 | tf_op jit(solution)/shard_map/ppermute | solution.py:21
  162.6 4.0 %collective-permute-start.20 = (bf16[192,512]{1,0:T(8,128)(2,1)S(1)}, bf16[192,512]{1,0:T(8,128)(2,1)S(1)}, u32[]{:S(2)}, u32[]{:S(2)}) collective-permute-start(bf16[192,512]{1,0:T(8,128)(2,1)S(1)} %broadcast_select_fusion.3.refs_0_), channel_id=1, source_target_pairs={{0,1},{1,0},{2,3},{3,2},{4,5},{5,4},{6,7},{7,6},{8,9},{9,8},{10,11... | collective-permute-start | bytes 589832 | tf_op jit(solution)/shard_map/ppermute | solution.py:21
